TPU v7x, 32 devices: a whole 2x2x4 slice. The times are simulated.
32 devices in a mesh: px: 8 (over z, core), py: 4 (over y, x).
Axes of the slice: x: 2, y: 2, z: 4, core: 2. Of those that a mesh axis runs over, the one named last changes fastest.
Arguments:
- objective_grad: float32 [2, 8, 128, 512], P(None, None, 'px', 'py'), may hold values from -6 to 6
- coefficients: float32 [3, 128, 512], P(None, 'px', 'py'), may hold values from 0.2 to 2
- inv_x: bfloat16 [128, 4, 1, 128, 128], P('px', 'py'), may hold values from 0 to 1
- inv_y: bfloat16 [8, 16, 4, 128, 128], P('px', 'py'), may hold values from 0 to 1
- perf_cell: int32 [8192], P(('px', 'py')), may hold values from 0 to 2047
- perf_owner: int32 [8192, 1], P(('px', 'py')), may hold values from 0 to 3; in each aligned block of 256 rows (0 to 255, 256 to 511, ...) at most 128 rows name the same one
- perf_tile: float32 [2, 8192], P(None, ('px', 'py')), may hold values from -6 to 6
- perf_weight: float32 [8, 8192], P(None, ('px', 'py')), may hold values from -6 to 6
Outputs:
- adjoint: float32 [2, 8, 128, 512], P(None, None, 'px', 'py')
Inputs may be any that keep to these rules, and one draw needn't show every extreme that they name: `perf_owner`: among the records of one block at most 128 name the same owner, and in some block one owner is named exactly 128 times.
All inputs are finite; a program needn't handle non-finite values.
Results may differ from a plain program's by a relative error of at most 0.00092.
Values may be sent and summed in bfloat16 or wider, within the bound.
A program may use at most 64 MiB of HBM per device.

v0:
```python
import functools

import jax
import jax.numpy as jnp
from jax import lax
from jax.experimental import pallas as pl
from jax.experimental.pallas import tpu as pltpu
from jax.sharding import PartitionSpec as P


def passed_along(value, axis, steps):
    count = lax.axis_size(axis)
    leading, last = (max(0, -steps), min(count, count - steps))
    return lax.ppermute(value, axis, [(source, source + steps) for source in range(leading, last)])


def extended(cells, sides, width):
    for axis, dim in sides:
        count = lax.axis_size(axis)
        ends = count - 1
        head = lax.slice_in_dim(cells, 0, width, axis=dim)
        tail = lax.slice_in_dim(cells, cells.shape[dim] - width, cells.shape[dim], axis=dim)
        cells = jnp.concatenate(
            [
                lax.ppermute(tail, axis, [(i, (i + 1) % count) for i in range(ends)]),
                cells,
                lax.ppermute(head, axis, [((i + 1) % count, i) for i in range(ends)]),
            ],
            axis=dim,
        )
    return cells


def shards(
    objective_grad, coefficients, inv_x, inv_y, perf_cell, perf_owner, perf_tile, perf_weight
):
    objectives = objective_grad.shape[1]
    width_x = coefficients.shape[1]
    width_y = coefficients.shape[2]
    storage = coefficients[0]
    conduct_x = coefficients[1]
    conduct_y = coefficients[2]
    below_x = passed_along(conduct_x[-1:, :], "px", 1)
    below_y = passed_along(conduct_y[:, -1:], "py", 1)
    lower_x = jnp.concatenate([below_x, conduct_x[:-1, :]], 0)
    lower_y = jnp.concatenate([below_y, conduct_y[:, :-1]], 1)
    diagonal = storage + conduct_x + lower_x + conduct_y + lower_y
    segment = inv_x.shape[3]
    blocks_x = inv_x.reshape(inv_x.shape[0], inv_x.shape[2], segment, segment)
    blocks_y = inv_y.reshape(inv_y.shape[1], inv_y.shape[2], segment, segment)

    def operate(iterate):
        padded = extended(iterate, (("px", 1), ("py", 2)), 1)
        return (
            diagonal * iterate
            - conduct_x * padded[:, 2:, 1:-1]
            - lower_x * padded[:, :-2, 1:-1]
            - conduct_y * padded[:, 1:-1, 2:]
            - lower_y * padded[:, 1:-1, :-2]
        )

    def relax_first(residual):
        turned = jnp.swapaxes(residual.astype(jnp.bfloat16), 1, 2)
        line_rows = lax.all_to_all(turned, "px", split_axis=1, concat_axis=2, tiled=True)
        shaped = line_rows.reshape(objectives, line_rows.shape[1], -1, segment)
        update = jnp.einsum("rkij,qrkj->qrki", blocks_x, shaped, preferred_element_type=jnp.float32)
        returned = lax.all_to_all(
            update.reshape(line_rows.shape), "px", split_axis=2, concat_axis=1, tiled=True
        )
        return jnp.swapaxes(returned, 1, 2)

    def relax_second(residual):
        line_rows = lax.all_to_all(
            residual.astype(jnp.bfloat16), "py", split_axis=1, concat_axis=2, tiled=True
        )
        shaped = line_rows.reshape(objectives, line_rows.shape[1], -1, segment)
        update = jnp.einsum("xkij,qxkj->qxki", blocks_y, shaped, preferred_element_type=jnp.float32)
        return lax.all_to_all(
            update.reshape(line_rows.shape), "py", split_axis=2, concat_axis=1, tiled=True
        )

    def relaxed_solve(right_side):
        iterate = relax_first(right_side)
        iterate = iterate + relax_second(right_side - operate(iterate))
        iterate = iterate + relax_first(right_side - operate(iterate))
        iterate = iterate + relax_second(right_side - operate(iterate))
        return iterate

    records = perf_cell.shape[0]
    owners = lax.axis_size("py")
    capacity = 2 * records // owners
    payload = jnp.concatenate([perf_tile, perf_weight, perf_cell.astype(jnp.float32)[None, :]], 0)
    owner_index = perf_owner[:, 0]
    onehot = (owner_index[:, None] == jnp.arange(owners, dtype=jnp.int32)[None, :]).astype(
        jnp.int32
    )
    rank_in_owner = jnp.sum((jnp.cumsum(onehot, 0) - 1) * onehot, axis=1)
    slot_index = owner_index * capacity + rank_in_owner
    packed = (
        jnp.zeros((payload.shape[0], owners * capacity), jnp.float32).at[:, slot_index].set(payload)
    )
    arrived = lax.all_to_all(packed, "py", split_axis=1, concat_axis=1, tiled=True)
    tile_rows = arrived[0:2]
    weight_rows = arrived[2 : 2 + objectives]
    cell_index = arrived[2 + objectives].astype(jnp.int32)
    values = tile_rows[:, None, :] * weight_rows[None, :, :]
    well_loads = (
        jnp.zeros((2, objectives, width_x * width_y), jnp.float32).at[:, :, cell_index].add(values)
    )
    well_loads = well_loads.reshape(2, objectives, width_x, width_y)
    second_adjoint = relaxed_solve(objective_grad[1] + well_loads[1])
    first_adjoint = relaxed_solve(objective_grad[0] + well_loads[0] + storage * second_adjoint)
    return jnp.stack([first_adjoint, second_adjoint])


MESH = pl.DeviceIdType.MESH
DIAG, COND_X, LOW_X, COND_Y, LOW_Y, STORE = range(6)
B_TO_LINES, Z1_TO_CELLS, Z2_TO_LINES, Z3_TO_CELLS = range(4)
COEF = 8


def swap_bits(tiles, tile_bit, shift, lane):
    keep = (lane & shift) == 0
    width = lane.shape[1]
    out = list(tiles)
    for a in range(len(tiles)):
        if a & tile_bit:
            continue
        b = a | tile_bit
        out[a] = jnp.where(keep, tiles[a], pltpu.roll(tiles[b], shift, 1))
        out[b] = jnp.where(keep, pltpu.roll(tiles[a], width - shift, 1), tiles[b])
    return out


def fused(
    n_px, n_py, cells_x,
    grad, coef, inv_x, inv_y, cell, owner, tile, weight,
    out,
    sent, got, edge_sent, edge_got, sent_far, lines_far, cells_far, records, near_x, near_y, coef_cells, coef_lines, blocks_y, loads,
    send_sem, recv_sem, edge_send, edge_recv, far_send, far_recv, rec_send, rec_recv, near_send, near_recv, inv_send, inv_recv, inv_own,
):
    me = lax.axis_index("px")
    mk = lax.axis_index("py")
    after_k, before_k = lax.rem(mk + 1, n_py), lax.rem(mk + n_py - 1, n_py)
    objectives, width = weight.shape[0], coef.shape[2]
    parts = cells_x // n_px
    last = cells_x - 1
    per_y = inv_y.shape[0]
    lane = lax.broadcasted_iota(jnp.int32, (objectives, width), 1)
    group = lane // cells_x
    sub = lax.broadcasted_iota(jnp.int32, (objectives, width), 0)

    def remote(source, target, sems, where):
        return pltpu.make_async_remote_copy(
            src_ref=source, dst_ref=target, send_sem=sems[0], recv_sem=sems[1],
            device_id=where, device_id_type=MESH,
        )

    def await_bytes(ref, sem):
        pltpu.make_async_copy(ref, ref, sem).wait()

    def swap_axes(tiles):
        bit = 1
        while bit < cells_x:
            tiles = swap_bits(tiles, bit, bit, lane)
            bit *= 2
        return tiles

    def swap_blocks(tiles):
        bit = 1
        while bit < n_px:
            tiles = swap_bits(tiles, bit, bit * cells_x, lane)
            bit *= 2
        return tiles

    def shifted(value, groups):
        amount = (groups * cells_x) % width
        return value if amount == 0 else pltpu.roll(value, amount, 1)

    def swap_rows(value, lane_bit, row_bit):
        low_lane, low_row = (lane & lane_bit) == 0, (sub & row_bit) == 0
        onward = pltpu.roll(pltpu.roll(value, row_bit, 0), width - lane_bit, 1)
        backward = pltpu.roll(pltpu.roll(value, objectives - row_bit, 0), lane_bit, 1)
        return jnp.where(low_lane == low_row, value, jnp.where(low_row, backward, onward))

    def turn_edges(up, down):
        pair = swap_bits([up, down], 1, cells_x, lane)
        return [swap_rows(swap_rows(t, 4 * cells_x, 4), 2 * cells_x, 2) for t in pair]

    def send(phase, tiles, edges, to_lines):
        turned = swap_axes(tiles)
        packed = swap_blocks(turned)
        for p in range(n_px):
            for part in range(parts):
                sent[phase, p, part] = packed[part * n_px + p]
        if edges:
            up = jnp.where(group == 0, 0.0, shifted(turned[last], 1))
            down = jnp.where(group == n_px - 1, 0.0, shifted(turned[0], -1))
            pair = turn_edges(up, down)
            for p in range(n_px):
                row = p // 2 * 2
                edge_sent[phase, p] = pair[p % 2][row : row + 2]
            if to_lines:
                sent_far[phase, 0] = pltpu.roll(turned[last], lax.rem(me + 1, n_px) * cells_x, 1)
                sent_far[phase, 1] = pltpu.roll(turned[0], me * cells_x, 1)
            else:
                sent_far[phase, 0] = tiles[last]
                sent_far[phase, 1] = tiles[0]
            for copy, here in far_copies(phase, to_lines):
                @pl.when(here)
                def _():
                    copy.start()
        for d in range(1, n_px):
            to = lax.rem(me + d, n_px)
            remote(
                sent.at[phase, to], got.at[phase, me], (send_sem.at[phase], recv_sem.at[phase]), (to, mk)
            ).start()
            if edges:
                remote(
                    edge_sent.at[phase, to], edge_got.at[phase, me],
                    (edge_send.at[phase], edge_recv.at[phase]), (to, mk),
                ).start()
        got[phase, me] = sent[phase, me]
        if edges:
            edge_got[phase, me] = edge_sent[phase, me]

    def far_copies(phase, to_lines):
        index = phase // 2
        copies = []
        sems = [(far_send.at[phase, d], far_recv.at[phase, d]) for d in range(2)]
        if to_lines:
            copies.append((remote(sent_far.at[phase, 0], lines_far.at[index, 0, me], sems[0], (0, after_k)), mk + 1 < n_py))
            copies.append((remote(sent_far.at[phase, 1], lines_far.at[index, 1, me], sems[1], (n_px - 1, before_k)), mk > 0))
        else:
            for d in range(n_px):
                to = lax.rem(me + d, n_px)
                copies.append((remote(sent_far.at[phase, 0], cells_far.at[index, 0], sems[0], (to, after_k)), (me == n_px - 1) & (mk + 1 < n_py)))
                copies.append((remote(sent_far.at[phase, 1], cells_far.at[index, 1], sems[1], (to, before_k)), (me == 0) & (mk > 0)))
        return copies

    def receive(phase, edges, to_lines):
        await_bytes(got.at[phase, pl.ds(0, n_px - 1)], recv_sem.at[phase])
        tiles = swap_blocks([got[phase, p, part] for part in range(parts) for p in range(n_px)])
        if not edges:
            return tiles
        await_bytes(edge_got.at[phase, pl.ds(0, n_px - 1)], edge_recv.at[phase])
        up, down = turn_edges(
            *[jnp.concatenate([edge_got[phase, p] for p in range(first, n_px, 2)], 0) for first in range(2)]
        )
        index = phase // 2
        if to_lines:
            @pl.when((me == 0) & (mk > 0))
            def _():
                await_bytes(lines_far.at[index, 0], far_recv.at[phase, 0])

            @pl.when((me == n_px - 1) & (mk + 1 < n_py))
            def _():
                await_bytes(lines_far.at[index, 1], far_recv.at[phase, 1])

            far = []
            for d in range(2):
                value = lines_far[index, d, 0]
                for p in range(1, n_px):
                    value = jnp.where(group == p, lines_far[index, d, p], value)
                far.append(value)
            return tiles, up + far[0], down + far[1], None, None

        @pl.when(mk > 0)
        def _():
            await_bytes(cells_far.at[index, 0], far_recv.at[phase, 0])

        @pl.when(mk + 1 < n_py)
        def _():
            await_bytes(cells_far.at[index, 1], far_recv.at[phase, 1])

        back = lax.rem(n_px - me, n_px) * cells_x
        left = pltpu.roll(cells_far[index, 0], back, 1)
        right = pltpu.roll(cells_far[index, 1], back, 1)
        lefts = [left if x == 0 else pltpu.roll(left, width - x, 1) for x in range(cells_x)]
        rights = [pltpu.roll(right, width - 1 - x, 1) for x in range(cells_x)]
        return tiles, up, down, lefts, rights

    def residual(right_side, field, coefs, tile_next, tile_prev, lane_next, lane_prev):
        tiles, up, down, lefts, rights = field
        result = []
        for t in range(cells_x):
            z = tiles[t]
            before = up if t == 0 else tiles[t - 1]
            after = down if t == last else tiles[t + 1]
            left = jnp.where(lane == 0, 0.0 if lefts is None else lefts[t], pltpu.roll(z, 1, 1))
            right = jnp.where(lane == width - 1, 0.0 if rights is None else rights[t], pltpu.roll(z, width - 1, 1))

            def c(row):
                return coefs[t, pl.ds(row, 1), :]

            applied = c(DIAG) * z - c(tile_next) * after - c(tile_prev) * before - c(lane_next) * right - c(lane_prev) * left
            result.append(right_side[t] - applied)
        return result

    def relax(blocks, res):
        return [
            lax.dot_general(
                res[t].astype(jnp.bfloat16), blocks[t], (((1,), (1,)), ((), ())),
                preferred_element_type=jnp.float32,
            )
            for t in range(cells_x)
        ]

    lines_far[...] = jnp.zeros_like(lines_far)
    cells_far[...] = jnp.zeros_like(cells_far)
    records[mk, pl.ds(0, objectives)] = weight[...]
    records[mk, pl.ds(objectives, 2)] = tile[...]
    records[mk, pl.ds(objectives + 2, 1)] = cell[...].astype(jnp.float32)
    records[mk, pl.ds(objectives + 3, 1)] = owner[...].astype(jnp.float32)
    devices = n_px * n_py
    barrier = pltpu.get_barrier_semaphore()
    for d in range(1, devices):
        other = (lax.rem(me + d // n_py, n_px), lax.rem(mk + d % n_py, n_py))
        pl.semaphore_signal(barrier, inc=1, device_id=other, device_id_type=MESH)
    pl.semaphore_wait(barrier, devices - 1)

    def record_copy(d):
        return remote(records.at[mk], records.at[mk], (rec_send, rec_recv), (me, lax.rem(mk + d, n_py)))

    def block_copy(d):
        to = lax.rem(mk + d, n_py)
        return remote(
            inv_y.at[:, to], blocks_y.at[pl.ds(mk * per_y, per_y)], (inv_send, inv_recv), (me, to)
        )

    own_blocks = pltpu.make_async_copy(inv_y.at[:, mk], blocks_y.at[pl.ds(mk * per_y, per_y)], inv_own)
    copy_x = remote(coef.at[1], near_x, (near_send.at[0], near_recv.at[0]), (lax.rem(me + 1, n_px), mk))
    copy_y = remote(coef.at[2], near_y, (near_send.at[1], near_recv.at[1]), (me, after_k))
    has_x, has_y = me + 1 < n_px, mk + 1 < n_py
    for d in range(1, n_py):
        record_copy(d).start()
    pl.when(has_x)(lambda: copy_x.start())
    pl.when(has_y)(lambda: copy_y.start())
    own_blocks.start()

    count = weight.shape[1]
    x_number = lax.broadcasted_iota(jnp.int32, (cells_x, objectives, count), 0).astype(jnp.float32)
    y_number = lax.broadcasted_iota(jnp.int32, (width, count), 0).astype(jnp.float32)
    total = jnp.zeros((4 * cells_x * objectives, width), jnp.float32)
    for d in range(n_py):
        source = lax.rem(mk + d, n_py)
        if d == 1:
            await_bytes(records.at[pl.ds(0, n_py - 1)], rec_recv)
            for step in range(1, n_py):
                block_copy(step).start()
        cells = records[source, pl.ds(objectives + 2, 1)]
        owners = records[source, pl.ds(objectives + 3, 1)]
        at_x = jnp.floor(cells * (1.0 / width))
        at_y = cells - at_x * width
        at_x = jnp.where(owners == mk.astype(jnp.float32), at_x, -1.0)
        hit = x_number == at_x[None]
        spread = (y_number == at_y).astype(jnp.float32).astype(jnp.bfloat16)
        rows = []
        for s in range(2):
            value = records[source, pl.ds(objectives + s, 1)] * records[source, pl.ds(0, objectives)]
            high = value.astype(jnp.bfloat16).astype(jnp.float32)
            for piece in (high, value - high):
                rows.append(
                    jnp.where(hit, piece[None], 0.0).reshape(cells_x * objectives, count).astype(jnp.bfloat16)
                )
        total = total + lax.dot_general(
            jnp.concatenate(rows, 0), spread, (((1,), (1,)), ((), ())), preferred_element_type=jnp.float32
        )
    span = cells_x * objectives
    for s in range(2):
        loads[s] = total[2 * s * span : (2 * s + 1) * span] + total[(2 * s + 1) * span : (2 * s + 2) * span]

    def loaded(s):
        return [
            grad[s, :, t, :] + loads[s, pl.ds(t * objectives, objectives), :]
            for t in range(cells_x)
        ]

    def solve(base, right_side):
        send(base + B_TO_LINES, right_side, False, True)
        if base == 0:
            share_coefficients()
        line_side = receive(base + B_TO_LINES, False, True)
        send(base + Z1_TO_CELLS, relax(inv_x, line_side), True, False)
        field = receive(base + Z1_TO_CELLS, True, False)
        res = residual(right_side, field, coef_cells, COND_X, LOW_X, COND_Y, LOW_Y)
        if base == 0:
            await_bytes(blocks_y.at[pl.ds(0, per_y * (n_py - 1))], inv_recv)
            own_blocks.wait()
        update = relax(blocks_y, res)
        send(base + Z2_TO_LINES, [z + u for z, u in zip(field[0], update)], True, True)
        field = receive(base + Z2_TO_LINES, True, True)
        if base == 0:
            for t, value in enumerate(receive(COEF, False, True)):
                coef_lines[t] = value
        update = relax(inv_x, residual(line_side, field, coef_lines, COND_Y, LOW_Y, COND_X, LOW_X))
        send(base + Z3_TO_CELLS, [z + u for z, u in zip(field[0], update)], True, False)
        field = receive(base + Z3_TO_CELLS, True, False)
        update = relax(blocks_y, residual(right_side, field, coef_cells, COND_X, LOW_X, COND_Y, LOW_Y))
        return [z + u for z, u in zip(field[0], update)]

    def share_coefficients():
        storage, conduct_x, conduct_y = coef[0], coef[1], coef[2]
        pl.when(me > 0)(lambda: await_bytes(near_x, near_recv.at[0]))
        pl.when(mk > 0)(lambda: await_bytes(near_y, near_recv.at[1]))
        row = lax.broadcasted_iota(jnp.int32, conduct_x.shape, 0)
        column = lax.broadcasted_iota(jnp.int32, conduct_x.shape, 1)
        below_x = jnp.where(me > 0, pltpu.roll(near_x[...], 1, 0), 0.0)
        below_y = jnp.where(mk > 0, pltpu.roll(near_y[...], 1, 1), 0.0)
        lower_x = jnp.where(row == 0, below_x, pltpu.roll(conduct_x, 1, 0))
        lower_y = jnp.where(column == 0, below_y, pltpu.roll(conduct_y, 1, 1))
        diagonal = storage + conduct_x + lower_x + conduct_y + lower_y
        tiles = []
        for t in range(cells_x):
            value = jnp.zeros((objectives, width), jnp.float32)
            for number, array in enumerate((diagonal, conduct_x, lower_x, conduct_y, lower_y, storage)):
                value = jnp.where(sub == number, array[t : t + 1], value)
            coef_cells[t] = value
            tiles.append(value)
        send(COEF, tiles, False, True)

    def keep(s, tiles):
        for t in range(cells_x):
            out[s, :, t, :] = tiles[t]

    second = solve(0, loaded(1))
    keep(1, second)
    first_side = [b + coef_cells[t, pl.ds(STORE, 1), :] * second[t] for t, b in enumerate(loaded(0))]
    keep(0, solve(4, first_side))

    for phase in range(9):
        edges = phase != COEF and phase % 4 != B_TO_LINES
        await_bytes(sent.at[phase, pl.ds(0, n_px - 1)], send_sem.at[phase])
        if edges:
            await_bytes(edge_sent.at[phase, pl.ds(0, n_px - 1)], edge_send.at[phase])
            for copy, here in far_copies(phase, phase % 4 == Z2_TO_LINES):
                @pl.when(here)
                def _():
                    copy.wait_send()
    await_bytes(records.at[pl.ds(0, n_py - 1)], rec_send)
    await_bytes(blocks_y.at[pl.ds(0, per_y * (n_py - 1))], inv_send)
    pl.when(has_x)(lambda: copy_x.wait_send())
    pl.when(has_y)(lambda: copy_y.wait_send())


def fused_shards(
    objective_grad, coefficients, inv_x, inv_y, perf_cell, perf_owner, perf_tile, perf_weight
):
    steps, objectives, cells_x, width = objective_grad.shape
    n_px, n_py = lax.axis_size("px"), lax.axis_size("py")
    segment = inv_x.shape[3]
    records = perf_cell.shape[0]
    parts = cells_x // n_px
    f32 = jnp.float32
    dma = pltpu.SemaphoreType.DMA
    vmem = pl.BlockSpec(memory_space=pltpu.VMEM)
    anywhere = pl.BlockSpec(memory_space=pl.ANY)
    tile = (objectives, width)
    result = pl.pallas_call(
        functools.partial(fused, n_px, n_py, cells_x),
        out_shape=jax.ShapeDtypeStruct(objective_grad.shape, f32),
        in_specs=[vmem, vmem, vmem, anywhere, vmem, vmem, vmem, vmem],
        out_specs=vmem,
        scratch_shapes=[
            pltpu.VMEM((9, n_px, parts) + tile, f32),
            pltpu.VMEM((9, n_px, parts) + tile, f32),
            pltpu.VMEM((9, n_px, 2, width), f32),
            pltpu.VMEM((9, n_px, 2, width), f32),
            pltpu.VMEM((8, 2) + tile, f32),
            pltpu.VMEM((4, 2, n_px) + tile, f32),
            pltpu.VMEM((4, 2) + tile, f32),
            pltpu.VMEM((n_py, 2 * objectives, records), f32),
            pltpu.VMEM((cells_x, width), f32),
            pltpu.VMEM((cells_x, width), f32),
            pltpu.VMEM((cells_x,) + tile, f32),
            pltpu.VMEM((cells_x,) + tile, f32),
            pltpu.VMEM((cells_x, segment, segment), jnp.bfloat16),
            pltpu.VMEM((steps, objectives * cells_x, width), f32),
            dma((9,)), dma((9,)), dma((9,)), dma((9,)), dma((8, 2)), dma((8, 2)),
            dma, dma, dma((2,)), dma((2,)), dma, dma, dma,
        ],
        compiler_params=pltpu.CompilerParams(collective_id=0, has_side_effects=True),
    )(
        objective_grad,
        coefficients,
        inv_x.reshape(inv_x.shape[0], segment, segment),
        inv_y.reshape(inv_y.shape[1:]),
        perf_cell.reshape(1, records),
        perf_owner.reshape(1, records),
        perf_tile,
        perf_weight,
    )
    return result


def per_device(*args):
    grad, inv_x = args[0], args[2]
    objectives, cells_x, width = grad.shape[1:]
    n_px = lax.axis_size("px")
    fits = (
        inv_x.shape[2] == 1
        and width == inv_x.shape[3] == 128
        and cells_x * n_px == width
        and inv_x.shape[0] == cells_x
        and cells_x % n_px == 0
        and n_px == objectives == 8
    )
    return fused_shards(*args) if fits else shards(*args)


def solution(mesh):
    return jax.shard_map(
        per_device,
        mesh=mesh,
        in_specs=(
            P(None, None, "px", "py"),
            P(None, "px", "py"),
            P("px", "py", None, None, None),
            P("px", "py", None, None, None),
            P(("px", "py")),
            P(("px", "py"), None),
            P(None, ("px", "py")),
            P(None, ("px", "py")),
        ),
        out_specs=P(None, None, "px", "py"),
        check_vma=False,
    )
```

profile of v0, /device:TPU:0, one launch (start us, length us, event | category | flops | bytes accessed | tf_op | source)
XLA Modules:
  0.0 56.3 jit_solution(496956407467407987)
XLA Ops:
  0.0 54.7 %shard_map.82 = f32[2,8,16,128]{3,2,1,0:T(8,128)} custom-call(f32[2,8,16,128]{3,2,1,0:T(8,128)} %grad.1, f32[3,16,128]{2,1,0:T(8,128)} %coef.1, bf16[16,128,128]{2,1,0:T(8,128)(2,1)} %bitcast.4, bf16[4,4,128,128]{3,2,1,0:T(8,128)(2,1)} %bitcast.5, s32[1,256]{1,0:T(1,128)} %bitcast.6, s32[1,256]{1,0:T(1,128)} %bitcast.7, f32[2,256]{1,0:T(2,128)} %tile.1, ...), custom_call_target="tpu_custom_call" | custom-call | tf_op jit(solution)/shard_map/pallas_call | solution.py:459
  54.7 1.6 %copy.10 = f32[2,8,16,128]{3,2,1,0:T(8,128)} copy(f32[2,8,16,128]{3,2,1,0:T(8,128)} %shard_map.82) | data formatting | bytes 262144
where the time goes:
time: 56.4 us; the launch traced here: 56.3 us
  Pallas kernels  54.7 us (97%)
  local copies, waits for them, and re-layouts  1.57 us (3%)
    pallas_call x1, Pallas kernels, fused_shards(): pl.pallas_call(functools.partial(fused, n_px, n_py, cells_x), out_shape=j...  54.7 us
    unnamed x1, local copies, waits for them, and re-layouts  1.57 us

commit v1 on v0

--- a/solution.py
+++ b/solution.py
@@ -136,8 +136,9 @@
     n_px, n_py, cells_x,
     grad, coef, inv_x, inv_y, cell, owner, tile, weight,
     out,
-    sent, got, edge_sent, edge_got, sent_far, lines_far, cells_far, records, near_x, near_y, coef_cells, coef_lines, blocks_y, loads,
-    send_sem, recv_sem, edge_send, edge_recv, far_send, far_recv, rec_send, rec_recv, near_send, near_recv, inv_send, inv_recv, inv_own,
+    sent, got, sent_far, lines_far, cells_far, records, near_x, near_y, coef_cells, coef_lines, blocks_y, loads,
+    grad_here, coef_here, blocks_x, cell_here, owner_here, tile_here,
+    send_sem, recv_sem, far_send, far_recv, rec_send, rec_recv, near_send, near_recv, inv_send, inv_recv, inv_own, load_sem,
 ):
     me = lax.axis_index("px")
     mk = lax.axis_index("py")
@@ -187,65 +188,81 @@
         pair = swap_bits([up, down], 1, cells_x, lane)
         return [swap_rows(swap_rows(t, 4 * cells_x, 4), 2 * cells_x, 2) for t in pair]
 
+    def peers():
+        low = me < n_px // 2
+        for i in range(n_px - 1):
+            down, up = n_px - 1 - i, i
+            down = jnp.where(down <= me, down - 1, down)
+            up = jnp.where(up >= me, up + 1, up)
+            yield jnp.where(low, down, up)
+
+    full = parts * objectives
+
+    def rows_of(edges):
+        return pl.ds(0, full + 2 if edges else full)
+
     def send(phase, tiles, edges, to_lines):
         turned = swap_axes(tiles)
         packed = swap_blocks(turned)
         for p in range(n_px):
             for part in range(parts):
-                sent[phase, p, part] = packed[part * n_px + p]
+                sent[phase, p, pl.ds(part * objectives, objectives)] = packed[part * n_px + p]
         if edges:
             up = jnp.where(group == 0, 0.0, shifted(turned[last], 1))
             down = jnp.where(group == n_px - 1, 0.0, shifted(turned[0], -1))
             pair = turn_edges(up, down)
             for p in range(n_px):
                 row = p // 2 * 2
-                edge_sent[phase, p] = pair[p % 2][row : row + 2]
+                sent[phase, p, pl.ds(full, 2)] = pair[p % 2][row : row + 2]
             if to_lines:
                 sent_far[phase, 0] = pltpu.roll(turned[last], lax.rem(me + 1, n_px) * cells_x, 1)
                 sent_far[phase, 1] = pltpu.roll(turned[0], me * cells_x, 1)
             else:
                 sent_far[phase, 0] = tiles[last]
                 sent_far[phase, 1] = tiles[0]
-            for copy, here in far_copies(phase, to_lines):
+            for copies, here in far_copies(phase, to_lines):
                 @pl.when(here)
                 def _():
-                    copy.start()
-        for d in range(1, n_px):
-            to = lax.rem(me + d, n_px)
+                    for copy in copies:
+                        copy.start()
+        rows = rows_of(edges)
+        for to in peers():
             remote(
-                sent.at[phase, to], got.at[phase, me], (send_sem.at[phase], recv_sem.at[phase]), (to, mk)
+                sent.at[phase, to, rows], got.at[phase, me, rows],
+                (send_sem.at[phase], recv_sem.at[phase]), (to, mk),
             ).start()
-            if edges:
-                remote(
-                    edge_sent.at[phase, to], edge_got.at[phase, me],
-                    (edge_send.at[phase], edge_recv.at[phase]), (to, mk),
-                ).start()
-        got[phase, me] = sent[phase, me]
-        if edges:
-            edge_got[phase, me] = edge_sent[phase, me]
+        got[phase, me, rows] = sent[phase, me, rows]
 
     def far_copies(phase, to_lines):
         index = phase // 2
         copies = []
         sems = [(far_send.at[phase, d], far_recv.at[phase, d]) for d in range(2)]
         if to_lines:
-            copies.append((remote(sent_far.at[phase, 0], lines_far.at[index, 0, me], sems[0], (0, after_k)), mk + 1 < n_py))
-            copies.append((remote(sent_far.at[phase, 1], lines_far.at[index, 1, me], sems[1], (n_px - 1, before_k)), mk > 0))
+            copies.append(([remote(sent_far.at[phase, 0], lines_far.at[index, 0, me], sems[0], (0, after_k))], mk + 1 < n_py))
+            copies.append(([remote(sent_far.at[phase, 1], lines_far.at[index, 1, me], sems[1], (n_px - 1, before_k))], mk > 0))
         else:
-            for d in range(n_px):
-                to = lax.rem(me + d, n_px)
-                copies.append((remote(sent_far.at[phase, 0], cells_far.at[index, 0], sems[0], (to, after_k)), (me == n_px - 1) & (mk + 1 < n_py)))
-                copies.append((remote(sent_far.at[phase, 1], cells_far.at[index, 1], sems[1], (to, before_k)), (me == 0) & (mk > 0)))
+            copies.append((
+                [remote(sent_far.at[phase, 0], cells_far.at[index, 0], sems[0], (d, after_k)) for d in range(n_px)],
+                (me == n_px - 1) & (mk + 1 < n_py),
+            ))
+            copies.append((
+                [remote(sent_far.at[phase, 1], cells_far.at[index, 1], sems[1], (d, before_k)) for d in range(n_px)],
+                (me == 0) & (mk > 0),
+            ))
         return copies
 
     def receive(phase, edges, to_lines):
-        await_bytes(got.at[phase, pl.ds(0, n_px - 1)], recv_sem.at[phase])
-        tiles = swap_blocks([got[phase, p, part] for part in range(parts) for p in range(n_px)])
+        await_bytes(got.at[phase, pl.ds(0, n_px - 1), rows_of(edges)], recv_sem.at[phase])
+        tiles = swap_blocks(
+            [got[phase, p, pl.ds(part * objectives, objectives)] for part in range(parts) for p in range(n_px)]
+        )
         if not edges:
             return tiles
-        await_bytes(edge_got.at[phase, pl.ds(0, n_px - 1)], edge_recv.at[phase])
         up, down = turn_edges(
-            *[jnp.concatenate([edge_got[phase, p] for p in range(first, n_px, 2)], 0) for first in range(2)]
+            *[
+                jnp.concatenate([got[phase, p, pl.ds(full, 2)] for p in range(first, n_px, 2)], 0)
+                for first in range(2)
+            ]
         )
         index = phase // 2
         if to_lines:
@@ -306,18 +323,23 @@
             for t in range(cells_x)
         ]
 
+    barrier = pltpu.get_barrier_semaphore()
+    for to in peers():
+        pl.semaphore_signal(barrier, inc=1, device_id=(to, mk), device_id_type=MESH)
+    for d in range(1, n_py):
+        pl.semaphore_signal(barrier, inc=1, device_id=(me, lax.rem(mk + d, n_py)), device_id_type=MESH)
+
+    pairs = (
+        (weight, records.at[mk, pl.ds(0, objectives)]), (tile, tile_here), (cell, cell_here), (owner, owner_here),
+        (coef, coef_here), (grad, grad_here), (inv_x, blocks_x),
+    )
+    fetches = [pltpu.make_async_copy(*pair, load_sem.at[i]) for i, pair in enumerate(pairs)]
+    for fetch in fetches:
+        fetch.start()
+    own_blocks = pltpu.make_async_copy(inv_y.at[:, mk], blocks_y.at[pl.ds(mk * per_y, per_y)], inv_own)
+    own_blocks.start()
     lines_far[...] = jnp.zeros_like(lines_far)
     cells_far[...] = jnp.zeros_like(cells_far)
-    records[mk, pl.ds(0, objectives)] = weight[...]
-    records[mk, pl.ds(objectives, 2)] = tile[...]
-    records[mk, pl.ds(objectives + 2, 1)] = cell[...].astype(jnp.float32)
-    records[mk, pl.ds(objectives + 3, 1)] = owner[...].astype(jnp.float32)
-    devices = n_px * n_py
-    barrier = pltpu.get_barrier_semaphore()
-    for d in range(1, devices):
-        other = (lax.rem(me + d // n_py, n_px), lax.rem(mk + d % n_py, n_py))
-        pl.semaphore_signal(barrier, inc=1, device_id=other, device_id_type=MESH)
-    pl.semaphore_wait(barrier, devices - 1)
 
     def record_copy(d):
         return remote(records.at[mk], records.at[mk], (rec_send, rec_recv), (me, lax.rem(mk + d, n_py)))
@@ -328,26 +350,16 @@
             inv_y.at[:, to], blocks_y.at[pl.ds(mk * per_y, per_y)], (inv_send, inv_recv), (me, to)
         )
 
-    own_blocks = pltpu.make_async_copy(inv_y.at[:, mk], blocks_y.at[pl.ds(mk * per_y, per_y)], inv_own)
-    copy_x = remote(coef.at[1], near_x, (near_send.at[0], near_recv.at[0]), (lax.rem(me + 1, n_px), mk))
-    copy_y = remote(coef.at[2], near_y, (near_send.at[1], near_recv.at[1]), (me, after_k))
+    copy_x = remote(coef_here.at[1], near_x, (near_send.at[0], near_recv.at[0]), (lax.rem(me + 1, n_px), mk))
+    copy_y = remote(coef_here.at[2], near_y, (near_send.at[1], near_recv.at[1]), (me, after_k))
     has_x, has_y = me + 1 < n_px, mk + 1 < n_py
-    for d in range(1, n_py):
-        record_copy(d).start()
-    pl.when(has_x)(lambda: copy_x.start())
-    pl.when(has_y)(lambda: copy_y.start())
-    own_blocks.start()
 
     count = weight.shape[1]
+    span = cells_x * objectives
     x_number = lax.broadcasted_iota(jnp.int32, (cells_x, objectives, count), 0).astype(jnp.float32)
     y_number = lax.broadcasted_iota(jnp.int32, (width, count), 0).astype(jnp.float32)
-    total = jnp.zeros((4 * cells_x * objectives, width), jnp.float32)
-    for d in range(n_py):
-        source = lax.rem(mk + d, n_py)
-        if d == 1:
-            await_bytes(records.at[pl.ds(0, n_py - 1)], rec_recv)
-            for step in range(1, n_py):
-                block_copy(step).start()
+
+    def loads_from(source, s):
         cells = records[source, pl.ds(objectives + 2, 1)]
         owners = records[source, pl.ds(objectives + 3, 1)]
         at_x = jnp.floor(cells * (1.0 / width))
@@ -355,33 +367,57 @@
         at_x = jnp.where(owners == mk.astype(jnp.float32), at_x, -1.0)
         hit = x_number == at_x[None]
         spread = (y_number == at_y).astype(jnp.float32).astype(jnp.bfloat16)
-        rows = []
-        for s in range(2):
-            value = records[source, pl.ds(objectives + s, 1)] * records[source, pl.ds(0, objectives)]
-            high = value.astype(jnp.bfloat16).astype(jnp.float32)
-            for piece in (high, value - high):
-                rows.append(
-                    jnp.where(hit, piece[None], 0.0).reshape(cells_x * objectives, count).astype(jnp.bfloat16)
-                )
-        total = total + lax.dot_general(
+        value = records[source, pl.ds(objectives + s, 1)] * records[source, pl.ds(0, objectives)]
+        high = value.astype(jnp.bfloat16).astype(jnp.float32)
+        rows = [
+            jnp.where(hit, piece[None], 0.0).reshape(span, count).astype(jnp.bfloat16)
+            for piece in (high, value - high)
+        ]
+        total = lax.dot_general(
             jnp.concatenate(rows, 0), spread, (((1,), (1,)), ((), ())), preferred_element_type=jnp.float32
         )
-    span = cells_x * objectives
+        return total[:span] + total[span:]
+
+    for fetch in fetches[:4]:
+        fetch.wait()
+    records[mk, pl.ds(objectives, 2)] = tile_here[...]
+    records[mk, pl.ds(objectives + 2, 1)] = cell_here[...].astype(jnp.float32)
+    records[mk, pl.ds(objectives + 3, 1)] = owner_here[...].astype(jnp.float32)
+    fetches[4].wait()
     for s in range(2):
-        loads[s] = total[2 * s * span : (2 * s + 1) * span] + total[(2 * s + 1) * span : (2 * s + 2) * span]
+        loads[s] = loads_from(mk, s)
+    pl.semaphore_wait(barrier, n_px + n_py - 2)
+    for d in range(1, n_py):
+        record_copy(d).start()
+    pl.when(has_x)(lambda: copy_x.start())
+    pl.when(has_y)(lambda: copy_y.start())
+    fetches[5].wait()
+    fetches[6].wait()
+    await_bytes(records.at[pl.ds(0, n_py - 1)], rec_recv)
+
+    def add_loads(s):
+        total = loads[s]
+        for d in range(1, n_py):
+            total = total + loads_from(lax.rem(mk + d, n_py), s)
+        loads[s] = total
+
+    add_loads(1)
 
     def loaded(s):
         return [
-            grad[s, :, t, :] + loads[s, pl.ds(t * objectives, objectives), :]
+            grad_here[s, :, t, :] + loads[s, pl.ds(t * objectives, objectives), :]
             for t in range(cells_x)
         ]
 
     def solve(base, right_side):
         send(base + B_TO_LINES, right_side, False, True)
         if base == 0:
+            for step in range(1, n_py):
+                block_copy(step).start()
             share_coefficients()
+            add_loads(0)
         line_side = receive(base + B_TO_LINES, False, True)
-        send(base + Z1_TO_CELLS, relax(inv_x, line_side), True, False)
+        send(base + Z1_TO_CELLS, relax(blocks_x, line_side), True, False)
         field = receive(base + Z1_TO_CELLS, True, False)
         res = residual(right_side, field, coef_cells, COND_X, LOW_X, COND_Y, LOW_Y)
         if base == 0:
@@ -393,14 +429,14 @@
         if base == 0:
             for t, value in enumerate(receive(COEF, False, True)):
                 coef_lines[t] = value
-        update = relax(inv_x, residual(line_side, field, coef_lines, COND_Y, LOW_Y, COND_X, LOW_X))
+        update = relax(blocks_x, residual(line_side, field, coef_lines, COND_Y, LOW_Y, COND_X, LOW_X))
         send(base + Z3_TO_CELLS, [z + u for z, u in zip(field[0], update)], True, False)
         field = receive(base + Z3_TO_CELLS, True, False)
         update = relax(blocks_y, residual(right_side, field, coef_cells, COND_X, LOW_X, COND_Y, LOW_Y))
         return [z + u for z, u in zip(field[0], update)]
 
     def share_coefficients():
-        storage, conduct_x, conduct_y = coef[0], coef[1], coef[2]
+        storage, conduct_x, conduct_y = coef_here[0], coef_here[1], coef_here[2]
         pl.when(me > 0)(lambda: await_bytes(near_x, near_recv.at[0]))
         pl.when(mk > 0)(lambda: await_bytes(near_y, near_recv.at[1]))
         row = lax.broadcasted_iota(jnp.int32, conduct_x.shape, 0)
@@ -430,13 +466,13 @@
 
     for phase in range(9):
         edges = phase != COEF and phase % 4 != B_TO_LINES
-        await_bytes(sent.at[phase, pl.ds(0, n_px - 1)], send_sem.at[phase])
+        await_bytes(sent.at[phase, pl.ds(0, n_px - 1), rows_of(edges)], send_sem.at[phase])
         if edges:
-            await_bytes(edge_sent.at[phase, pl.ds(0, n_px - 1)], edge_send.at[phase])
-            for copy, here in far_copies(phase, phase % 4 == Z2_TO_LINES):
+            for copies, here in far_copies(phase, phase % 4 == Z2_TO_LINES):
                 @pl.when(here)
                 def _():
-                    copy.wait_send()
+                    for copy in copies:
+                        copy.wait_send()
     await_bytes(records.at[pl.ds(0, n_py - 1)], rec_send)
     await_bytes(blocks_y.at[pl.ds(0, per_y * (n_py - 1))], inv_send)
     pl.when(has_x)(lambda: copy_x.wait_send())
@@ -458,14 +494,12 @@
     tile = (objectives, width)
     result = pl.pallas_call(
         functools.partial(fused, n_px, n_py, cells_x),
-        out_shape=jax.ShapeDtypeStruct(objective_grad.shape, f32),
-        in_specs=[vmem, vmem, vmem, anywhere, vmem, vmem, vmem, vmem],
+        out_shape=pltpu.VMEM(objective_grad.shape, f32),
+        in_specs=[anywhere] * 8,
         out_specs=vmem,
         scratch_shapes=[
-            pltpu.VMEM((9, n_px, parts) + tile, f32),
-            pltpu.VMEM((9, n_px, parts) + tile, f32),
-            pltpu.VMEM((9, n_px, 2, width), f32),
-            pltpu.VMEM((9, n_px, 2, width), f32),
+            pltpu.VMEM((9, n_px, (parts + 1) * objectives, width), f32),
+            pltpu.VMEM((9, n_px, (parts + 1) * objectives, width), f32),
             pltpu.VMEM((8, 2) + tile, f32),
             pltpu.VMEM((4, 2, n_px) + tile, f32),
             pltpu.VMEM((4, 2) + tile, f32),
@@ -476,8 +510,14 @@
             pltpu.VMEM((cells_x,) + tile, f32),
             pltpu.VMEM((cells_x, segment, segment), jnp.bfloat16),
             pltpu.VMEM((steps, objectives * cells_x, width), f32),
-            dma((9,)), dma((9,)), dma((9,)), dma((9,)), dma((8, 2)), dma((8, 2)),
-            dma, dma, dma((2,)), dma((2,)), dma, dma, dma,
+            pltpu.VMEM(objective_grad.shape, f32),
+            pltpu.VMEM(coefficients.shape, f32),
+            pltpu.VMEM((cells_x, segment, segment), jnp.bfloat16),
+            pltpu.VMEM((1, records), jnp.int32),
+            pltpu.VMEM((1, records), jnp.int32),
+            pltpu.VMEM((2, records), f32),
+            dma((9,)), dma((9,)), dma((8, 2)), dma((8, 2)),
+            dma, dma, dma((2,)), dma((2,)), dma, dma, dma, dma((7,)),
         ],
         compiler_params=pltpu.CompilerParams(collective_id=0, has_side_effects=True),
     )(

time: 56.4 us -> 51.6 us (0.915)
  Pallas kernels: 54.7 us -> 50.7 us
  local copies, waits for them, and re-layouts: 1.57 us -> 0.66 us
    pallas_call x1, Pallas kernels: 54.7 us -> 50.7 us  [fused_shards(): pl.pallas_call(functools.partial(fused, n_px, n_py, cells_x), out_shape=p...]
    unnamed x1, local copies, waits for them, and re-layouts: 1.57 us -> 0.66 us
where the time goes in v1:
time: 51.6 us; the launch traced here: 51.4 us
  Pallas kernels  50.7 us (98%)
  local copies, waits for them, and re-layouts  0.66 us (1%)
    pallas_call x1, Pallas kernels, fused_shards(): pl.pallas_call(functools.partial(fused, n_px, n_py, cells_x), out_shape=p...  50.7 us

profile of v1, /device:TPU:0, one launch (start us, length us, event | category | flops | bytes accessed | tf_op | source)
XLA Modules:
  0.0 51.4 jit_solution(6202160687841218198)
XLA Ops:
  0.0 50.7 %shard_map.82 = f32[2,8,16,128]{3,2,1,0:T(8,128)S(1)} custom-call(f32[2,8,16,128]{3,2,1,0:T(8,128)} %grad.1, f32[3,16,128]{2,1,0:T(8,128)} %coef.1, bf16[16,128,128]{2,1,0:T(8,128)(2,1)} %bitcast.4, bf16[4,4,128,128]{3,2,1,0:T(8,128)(2,1)} %bitcast.5, s32[1,256]{1,0:T(1,128)} %bitcast.6, s32[1,256]{1,0:T(1,128)} %bitcast.7, f32[2,256]{1,0:T(2,128)} %tile.1, ...), custom_call_target="tpu_custom_call" | custom-call | tf_op jit(solution)/shard_map/pallas_call | solution.py:495
  50.7 0.7 %copy.10 = f32[2,8,16,128]{3,2,1,0:T(8,128)} copy(f32[2,8,16,128]{3,2,1,0:T(8,128)S(1)} %shard_map.82) | data formatting | bytes 262144

commit v2 on v1

--- a/solution.py
+++ b/solution.py
@@ -119,16 +119,16 @@
 COEF = 8
 
 
-def swap_bits(tiles, tile_bit, shift, lane):
-    keep = (lane & shift) == 0
-    width = lane.shape[1]
-    out = list(tiles)
-    for a in range(len(tiles)):
-        if a & tile_bit:
-            continue
-        b = a | tile_bit
-        out[a] = jnp.where(keep, tiles[a], pltpu.roll(tiles[b], shift, 1))
-        out[b] = jnp.where(keep, pltpu.roll(tiles[a], width - shift, 1), tiles[b])
+def skewed_swap(tiles, step, lane):
+    count, width = len(tiles), lane.shape[1]
+    digit = (lane // step) % count
+    moved = [t if i == 0 else pltpu.roll(t, i * step % width, 1) for i, t in enumerate(tiles)]
+    out = [moved[-i % count] for i in range(count)]
+    bit = 1
+    while bit < count:
+        on = (digit & bit) != 0
+        out = [jnp.where(on, out[(i - bit) % count], out[i]) for i in range(count)]
+        bit *= 2
     return out
 
 
@@ -149,6 +149,8 @@
     per_y = inv_y.shape[0]
     lane = lax.broadcasted_iota(jnp.int32, (objectives, width), 1)
     group = lane // cells_x
+    digit = lane % n_px
+    ring = lane // n_px
     sub = lax.broadcasted_iota(jnp.int32, (objectives, width), 0)
 
     def remote(source, target, sems, where):
@@ -160,33 +162,11 @@
     def await_bytes(ref, sem):
         pltpu.make_async_copy(ref, ref, sem).wait()
 
-    def swap_axes(tiles):
-        bit = 1
-        while bit < cells_x:
-            tiles = swap_bits(tiles, bit, bit, lane)
-            bit *= 2
-        return tiles
-
-    def swap_blocks(tiles):
-        bit = 1
-        while bit < n_px:
-            tiles = swap_bits(tiles, bit, bit * cells_x, lane)
-            bit *= 2
-        return tiles
-
-    def shifted(value, groups):
-        amount = (groups * cells_x) % width
-        return value if amount == 0 else pltpu.roll(value, amount, 1)
-
-    def swap_rows(value, lane_bit, row_bit):
-        low_lane, low_row = (lane & lane_bit) == 0, (sub & row_bit) == 0
-        onward = pltpu.roll(pltpu.roll(value, row_bit, 0), width - lane_bit, 1)
-        backward = pltpu.roll(pltpu.roll(value, objectives - row_bit, 0), lane_bit, 1)
-        return jnp.where(low_lane == low_row, value, jnp.where(low_row, backward, onward))
-
-    def turn_edges(up, down):
-        pair = swap_bits([up, down], 1, cells_x, lane)
-        return [swap_rows(swap_rows(t, 4 * cells_x, 4), 2 * cells_x, 2) for t in pair]
+    def rolled(value, amount):
+        return value if amount % width == 0 else pltpu.roll(value, amount % width, 1)
+
+    def exchanged(tiles, step):
+        return [rolled(t, -i * step) for i, t in enumerate(skewed_swap(tiles, step, lane))]
 
     def peers():
         low = me < n_px // 2
@@ -196,30 +176,53 @@
             up = jnp.where(up >= me, up + 1, up)
             yield jnp.where(low, down, up)
 
-    full = parts * objectives
+    full = 2 * parts * objectives
 
     def rows_of(edges):
-        return pl.ds(0, full + 2 if edges else full)
+        return pl.ds(0, full + objectives if edges else full)
 
     def send(phase, tiles, edges, to_lines):
-        turned = swap_axes(tiles)
-        packed = swap_blocks(turned)
+        zero = jnp.zeros((objectives, width), jnp.float32)
+        borders = None
+        if to_lines:
+            turned = exchanged(tiles, n_px)
+            packed = [[turned[parts * p + i] for i in range(parts)] for p in range(n_px)]
+            if edges:
+                borders = [
+                    jnp.where(
+                        digit == n_px - 1,
+                        zero if p == 0 else packed[p - 1][parts - 1],
+                        zero if p == n_px - 1 else packed[p + 1][0],
+                    )
+                    for p in range(n_px)
+                ]
+                sent_far[phase, 0] = turned[last]
+                sent_far[phase, 1] = turned[0]
+        else:
+            halves = [skewed_swap(tiles[i * n_px : (i + 1) * n_px], 1, lane) for i in range(parts)]
+            packed = [[rolled(halves[i][p], -p) for i in range(parts)] for p in range(n_px)]
+            borders = []
+            for p in range(n_px):
+                value = zero
+                if p > 0:
+                    high = jnp.where(
+                        ring == cells_x - 1, packed[p - 1][1], rolled(halves[0][p - 1], -(p - 1) - n_px)
+                    )
+                    value = jnp.where(ring >= cells_x - 2, high, value)
+                if p < n_px - 1:
+                    low = jnp.where(ring == 0, packed[p + 1][0], rolled(halves[1][p + 1], n_px - (p + 1)))
+                    value = jnp.where(ring <= 1, low, value)
+                borders.append(value)
+            sent_far[phase, 0] = tiles[last]
+            sent_far[phase, 1] = tiles[0]
         for p in range(n_px):
-            for part in range(parts):
-                sent[phase, p, pl.ds(part * objectives, objectives)] = packed[part * n_px + p]
+            value = jnp.concatenate(packed[p], 0)
+            high = value.astype(jnp.bfloat16)
+            sent[phase, p, pl.ds(0, full // 2)] = high
+            sent[phase, p, pl.ds(full // 2, full // 2)] = (value - high.astype(jnp.float32)).astype(jnp.bfloat16)
+            if edges:
+                sent[phase, p, pl.ds(full, objectives)] = borders[p].astype(jnp.bfloat16)
         if edges:
-            up = jnp.where(group == 0, 0.0, shifted(turned[last], 1))
-            down = jnp.where(group == n_px - 1, 0.0, shifted(turned[0], -1))
-            pair = turn_edges(up, down)
-            for p in range(n_px):
-                row = p // 2 * 2
-                sent[phase, p, pl.ds(full, 2)] = pair[p % 2][row : row + 2]
-            if to_lines:
-                sent_far[phase, 0] = pltpu.roll(turned[last], lax.rem(me + 1, n_px) * cells_x, 1)
-                sent_far[phase, 1] = pltpu.roll(turned[0], me * cells_x, 1)
-            else:
-                sent_far[phase, 0] = tiles[last]
-                sent_far[phase, 1] = tiles[0]
             for copies, here in far_copies(phase, to_lines):
                 @pl.when(here)
                 def _():
@@ -253,18 +256,21 @@
 
     def receive(phase, edges, to_lines):
         await_bytes(got.at[phase, pl.ds(0, n_px - 1), rows_of(edges)], recv_sem.at[phase])
-        tiles = swap_blocks(
-            [got[phase, p, pl.ds(part * objectives, objectives)] for part in range(parts) for p in range(n_px)]
-        )
+        blocks = []
+        for p in range(n_px):
+            value = got[phase, p, pl.ds(0, full // 2)].astype(jnp.float32)
+            value = value + got[phase, p, pl.ds(full // 2, full // 2)].astype(jnp.float32)
+            blocks.append([value[i * objectives : (i + 1) * objectives] for i in range(parts)])
+        if to_lines:
+            tiles = [t for i in range(parts) for t in exchanged([block[i] for block in blocks], 1)]
+        else:
+            tiles = exchanged([t for block in blocks for t in block], n_px)
         if not edges:
             return tiles
-        up, down = turn_edges(
-            *[
-                jnp.concatenate([got[phase, p, pl.ds(full, 2)] for p in range(first, n_px, 2)], 0)
-                for first in range(2)
-            ]
-        )
+        borders = [got[phase, p, pl.ds(full, objectives)].astype(jnp.float32) for p in range(n_px)]
         index = phase // 2
+        zero = jnp.zeros((objectives, width), jnp.float32)
+        up, down = zero, zero
         if to_lines:
             @pl.when((me == 0) & (mk > 0))
             def _():
@@ -274,13 +280,10 @@
             def _():
                 await_bytes(lines_far.at[index, 1], far_recv.at[phase, 1])
 
-            far = []
-            for d in range(2):
-                value = lines_far[index, d, 0]
-                for p in range(1, n_px):
-                    value = jnp.where(group == p, lines_far[index, d, p], value)
-                far.append(value)
-            return tiles, up + far[0], down + far[1], None, None
+            for p in range(n_px):
+                up = jnp.where(digit == p, rolled(borders[p] + lines_far[index, 0, p], p + 1 - n_px), up)
+                down = jnp.where(digit == p, rolled(borders[p] + lines_far[index, 1, p], p), down)
+            return tiles, up, down, None, None
 
         @pl.when(mk > 0)
         def _():
@@ -290,12 +293,26 @@
         def _():
             await_bytes(cells_far.at[index, 1], far_recv.at[phase, 1])
 
-        back = lax.rem(n_px - me, n_px) * cells_x
-        left = pltpu.roll(cells_far[index, 0], back, 1)
-        right = pltpu.roll(cells_far[index, 1], back, 1)
-        lefts = [left if x == 0 else pltpu.roll(left, width - x, 1) for x in range(cells_x)]
-        rights = [pltpu.roll(right, width - 1 - x, 1) for x in range(cells_x)]
+        for p in range(n_px):
+            up = jnp.where(group == p, rolled(borders[p], (p + 1) * cells_x), up)
+            down = jnp.where(group == p, rolled(borders[p], p * cells_x), down)
+        left, right = cells_far[index, 0], cells_far[index, 1]
+        lefts = [pltpu.roll(left, lax.rem(2 * width - x * n_px - me, width), 1) for x in range(cells_x)]
+        rights = [pltpu.roll(right, lax.rem(2 * width - 1 - x * n_px - me, width), 1) for x in range(cells_x)]
         return tiles, up, down, lefts, rights
+
+    def beside(z, t, lefts, rights):
+        if lefts is not None:
+            left = jnp.where(lane == 0, lefts[t], pltpu.roll(z, 1, 1))
+            right = jnp.where(lane == width - 1, rights[t], pltpu.roll(z, width - 1, 1))
+            return left, right
+        left = jnp.where(ring == 0, jnp.where(lane == 0, 0.0, pltpu.roll(z, n_px + 1, 1)), pltpu.roll(z, n_px, 1))
+        right = jnp.where(
+            ring == cells_x - 1,
+            jnp.where(lane == width - 1, 0.0, pltpu.roll(z, width - n_px - 1, 1)),
+            pltpu.roll(z, width - n_px, 1),
+        )
+        return left, right
 
     def residual(right_side, field, coefs, tile_next, tile_prev, lane_next, lane_prev):
         tiles, up, down, lefts, rights = field
@@ -304,8 +321,7 @@
             z = tiles[t]
             before = up if t == 0 else tiles[t - 1]
             after = down if t == last else tiles[t + 1]
-            left = jnp.where(lane == 0, 0.0 if lefts is None else lefts[t], pltpu.roll(z, 1, 1))
-            right = jnp.where(lane == width - 1, 0.0 if rights is None else rights[t], pltpu.roll(z, width - 1, 1))
+            left, right = beside(z, t, lefts, rights)
 
             def c(row):
                 return coefs[t, pl.ds(row, 1), :]
@@ -315,13 +331,24 @@
         return result
 
     def relax(blocks, res):
-        return [
-            lax.dot_general(
-                res[t].astype(jnp.bfloat16), blocks[t], (((1,), (1,)), ((), ())),
-                preferred_element_type=jnp.float32,
+        result = []
+        for t in range(0, cells_x, 2):
+            product = lax.dot_general(
+                jnp.concatenate(res[t : t + 2], 0).astype(jnp.bfloat16), blocks[pl.ds(t, 2)].reshape(2 * width, width),
+                (((1,), (1,)), ((), ())), preferred_element_type=jnp.float32,
             )
-            for t in range(cells_x)
-        ]
+            result += [product[:objectives, :width], product[objectives:, width:]]
+        return result
+
+    def reorder_blocks():
+        shape = (width, width)
+        row, column = lax.broadcasted_iota(jnp.int32, shape, 0), lax.broadcasted_iota(jnp.int32, shape, 1)
+        place = (column == (row % n_px) * cells_x + row // n_px).astype(jnp.float32).astype(jnp.bfloat16)
+        for t in range(cells_x):
+            value = lax.dot_general(
+                blocks_x[t], place, (((1,), (1,)), ((), ())), preferred_element_type=jnp.float32
+            ).astype(jnp.bfloat16)
+            blocks_x[t] = jnp.dot(place, value, preferred_element_type=jnp.float32).astype(jnp.bfloat16)
 
     barrier = pltpu.get_barrier_semaphore()
     for to in peers():
@@ -393,6 +420,7 @@
     pl.when(has_y)(lambda: copy_y.start())
     fetches[5].wait()
     fetches[6].wait()
+    reorder_blocks()
     await_bytes(records.at[pl.ds(0, n_py - 1)], rec_recv)
 
     def add_loads(s):
@@ -498,8 +526,8 @@
         in_specs=[anywhere] * 8,
         out_specs=vmem,
         scratch_shapes=[
-            pltpu.VMEM((9, n_px, (parts + 1) * objectives, width), f32),
-            pltpu.VMEM((9, n_px, (parts + 1) * objectives, width), f32),
+            pltpu.VMEM((9, n_px, 3 * parts * objectives, width), jnp.bfloat16),
+            pltpu.VMEM((9, n_px, 3 * parts * objectives, width), jnp.bfloat16),
             pltpu.VMEM((8, 2) + tile, f32),
             pltpu.VMEM((4, 2, n_px) + tile, f32),
             pltpu.VMEM((4, 2) + tile, f32),
@@ -542,7 +570,7 @@
         and width == inv_x.shape[3] == 128
         and cells_x * n_px == width
         and inv_x.shape[0] == cells_x
-        and cells_x % n_px == 0
+        and cells_x == 2 * n_px
         and n_px == objectives == 8
     )
     return fused_shards(*args) if fits else shards(*args)

time: 51.6 us -> 47.1 us (0.913)
  Pallas kernels: 50.7 us -> 46.2 us
    pallas_call x1, Pallas kernels: 50.7 us -> 46.2 us  [fused_shards(): pl.pallas_call(functools.partial(fused, n_px, n_py, cells_x), out_shape=p...]
where the time goes in v2:
time: 47.1 us; the launch traced here: 46.9 us
  Pallas kernels  46.2 us (98%)
  local copies, waits for them, and re-layouts  0.66 us (1%)
    pallas_call x1, Pallas kernels, fused_shards(): pl.pallas_call(functools.partial(fused, n_px, n_py, cells_x), out_shape=p...  46.2 us

profile of v2, /device:TPU:0, one launch (start us, length us, event | category | flops | bytes accessed | tf_op | source)
XLA Modules:
  0.0 46.9 jit_solution(244100482946900896)
XLA Ops:
  0.0 46.2 %shard_map.82 = f32[2,8,16,128]{3,2,1,0:T(8,128)S(1)} custom-call(f32[2,8,16,128]{3,2,1,0:T(8,128)} %grad.1, f32[3,16,128]{2,1,0:T(8,128)} %coef.1, bf16[16,128,128]{2,1,0:T(8,128)(2,1)} %bitcast.4, bf16[4,4,128,128]{3,2,1,0:T(8,128)(2,1)} %bitcast.5, s32[1,256]{1,0:T(1,128)} %bitcast.6, s32[1,256]{1,0:T(1,128)} %bitcast.7, f32[2,256]{1,0:T(2,128)} %tile.1, ...), custom_call_target="tpu_custom_call" | custom-call | tf_op jit(solution)/shard_map/pallas_call | solution.py:523
  46.2 0.7 %copy.10 = f32[2,8,16,128]{3,2,1,0:T(8,128)} copy(f32[2,8,16,128]{3,2,1,0:T(8,128)S(1)} %shard_map.82) | data formatting | bytes 262144

commit v3 on v2

--- a/solution.py
+++ b/solution.py
@@ -181,6 +181,15 @@
     def rows_of(edges):
         return pl.ds(0, full + objectives if edges else full)
 
+    def send_far(phase, after, before, to_lines):
+        sent_far[phase, 0] = after.astype(jnp.bfloat16)
+        sent_far[phase, 1] = before.astype(jnp.bfloat16)
+        for copies, here in far_copies(phase, to_lines):
+            @pl.when(here)
+            def _():
+                for copy in copies:
+                    copy.start()
+
     def send(phase, tiles, edges, to_lines):
         zero = jnp.zeros((objectives, width), jnp.float32)
         borders = None
@@ -188,6 +197,7 @@
             turned = exchanged(tiles, n_px)
             packed = [[turned[parts * p + i] for i in range(parts)] for p in range(n_px)]
             if edges:
+                send_far(phase, turned[last], turned[0], to_lines)
                 borders = [
                     jnp.where(
                         digit == n_px - 1,
@@ -196,9 +206,8 @@
                     )
                     for p in range(n_px)
                 ]
-                sent_far[phase, 0] = turned[last]
-                sent_far[phase, 1] = turned[0]
         else:
+            send_far(phase, tiles[last], tiles[0], to_lines)
             halves = [skewed_swap(tiles[i * n_px : (i + 1) * n_px], 1, lane) for i in range(parts)]
             packed = [[rolled(halves[i][p], -p) for i in range(parts)] for p in range(n_px)]
             borders = []
@@ -213,8 +222,6 @@
                     low = jnp.where(ring == 0, packed[p + 1][0], rolled(halves[1][p + 1], n_px - (p + 1)))
                     value = jnp.where(ring <= 1, low, value)
                 borders.append(value)
-            sent_far[phase, 0] = tiles[last]
-            sent_far[phase, 1] = tiles[0]
         for p in range(n_px):
             value = jnp.concatenate(packed[p], 0)
             high = value.astype(jnp.bfloat16)
@@ -222,12 +229,6 @@
             sent[phase, p, pl.ds(full // 2, full // 2)] = (value - high.astype(jnp.float32)).astype(jnp.bfloat16)
             if edges:
                 sent[phase, p, pl.ds(full, objectives)] = borders[p].astype(jnp.bfloat16)
-        if edges:
-            for copies, here in far_copies(phase, to_lines):
-                @pl.when(here)
-                def _():
-                    for copy in copies:
-                        copy.start()
         rows = rows_of(edges)
         for to in peers():
             remote(
@@ -249,13 +250,22 @@
                 (me == n_px - 1) & (mk + 1 < n_py),
             ))
             copies.append((
-                [remote(sent_far.at[phase, 1], cells_far.at[index, 1], sems[1], (d, before_k)) for d in range(n_px)],
+                [remote(sent_far.at[phase, 1], cells_far.at[index, 1], sems[1], (d, before_k)) for d in reversed(range(n_px))],
                 (me == 0) & (mk > 0),
             ))
         return copies
 
     def receive(phase, edges, to_lines):
+        index = phase // 2
         await_bytes(got.at[phase, pl.ds(0, n_px - 1), rows_of(edges)], recv_sem.at[phase])
+        if edges:
+            for d, there in enumerate((mk > 0, mk + 1 < n_py)):
+                far = lines_far.at[index, d] if to_lines else cells_far.at[index, d]
+                here = there & (me == (0, n_px - 1)[d]) if to_lines else there
+
+                @pl.when(here)
+                def _():
+                    await_bytes(far, far_recv.at[phase, d])
         blocks = []
         for p in range(n_px):
             value = got[phase, p, pl.ds(0, full // 2)].astype(jnp.float32)
@@ -268,35 +278,18 @@
         if not edges:
             return tiles
         borders = [got[phase, p, pl.ds(full, objectives)].astype(jnp.float32) for p in range(n_px)]
-        index = phase // 2
         zero = jnp.zeros((objectives, width), jnp.float32)
         up, down = zero, zero
         if to_lines:
-            @pl.when((me == 0) & (mk > 0))
-            def _():
-                await_bytes(lines_far.at[index, 0], far_recv.at[phase, 0])
-
-            @pl.when((me == n_px - 1) & (mk + 1 < n_py))
-            def _():
-                await_bytes(lines_far.at[index, 1], far_recv.at[phase, 1])
-
             for p in range(n_px):
-                up = jnp.where(digit == p, rolled(borders[p] + lines_far[index, 0, p], p + 1 - n_px), up)
-                down = jnp.where(digit == p, rolled(borders[p] + lines_far[index, 1, p], p), down)
+                up = jnp.where(digit == p, rolled(borders[p] + lines_far[index, 0, p].astype(jnp.float32), p + 1 - n_px), up)
+                down = jnp.where(digit == p, rolled(borders[p] + lines_far[index, 1, p].astype(jnp.float32), p), down)
             return tiles, up, down, None, None
-
-        @pl.when(mk > 0)
-        def _():
-            await_bytes(cells_far.at[index, 0], far_recv.at[phase, 0])
-
-        @pl.when(mk + 1 < n_py)
-        def _():
-            await_bytes(cells_far.at[index, 1], far_recv.at[phase, 1])
 
         for p in range(n_px):
             up = jnp.where(group == p, rolled(borders[p], (p + 1) * cells_x), up)
             down = jnp.where(group == p, rolled(borders[p], p * cells_x), down)
-        left, right = cells_far[index, 0], cells_far[index, 1]
+        left, right = [cells_far[index, d].astype(jnp.float32) for d in range(2)]
         lefts = [pltpu.roll(left, lax.rem(2 * width - x * n_px - me, width), 1) for x in range(cells_x)]
         rights = [pltpu.roll(right, lax.rem(2 * width - 1 - x * n_px - me, width), 1) for x in range(cells_x)]
         return tiles, up, down, lefts, rights
@@ -446,17 +439,16 @@
             add_loads(0)
         line_side = receive(base + B_TO_LINES, False, True)
         send(base + Z1_TO_CELLS, relax(blocks_x, line_side), True, False)
+        if base == 0:
+            for t, value in enumerate(receive(COEF, False, True)):
+                coef_lines[t] = value
+            await_bytes(blocks_y.at[pl.ds(0, per_y * (n_py - 1))], inv_recv)
+            own_blocks.wait()
         field = receive(base + Z1_TO_CELLS, True, False)
         res = residual(right_side, field, coef_cells, COND_X, LOW_X, COND_Y, LOW_Y)
-        if base == 0:
-            await_bytes(blocks_y.at[pl.ds(0, per_y * (n_py - 1))], inv_recv)
-            own_blocks.wait()
         update = relax(blocks_y, res)
         send(base + Z2_TO_LINES, [z + u for z, u in zip(field[0], update)], True, True)
         field = receive(base + Z2_TO_LINES, True, True)
-        if base == 0:
-            for t, value in enumerate(receive(COEF, False, True)):
-                coef_lines[t] = value
         update = relax(blocks_x, residual(line_side, field, coef_lines, COND_Y, LOW_Y, COND_X, LOW_X))
         send(base + Z3_TO_CELLS, [z + u for z, u in zip(field[0], update)], True, False)
         field = receive(base + Z3_TO_CELLS, True, False)
@@ -528,9 +520,9 @@
         scratch_shapes=[
             pltpu.VMEM((9, n_px, 3 * parts * objectives, width), jnp.bfloat16),
             pltpu.VMEM((9, n_px, 3 * parts * objectives, width), jnp.bfloat16),
-            pltpu.VMEM((8, 2) + tile, f32),
-            pltpu.VMEM((4, 2, n_px) + tile, f32),
-            pltpu.VMEM((4, 2) + tile, f32),
+            pltpu.VMEM((8, 2) + tile, jnp.bfloat16),
+            pltpu.VMEM((4, 2, n_px) + tile, jnp.bfloat16),
+            pltpu.VMEM((4, 2) + tile, jnp.bfloat16),
             pltpu.VMEM((n_py, 2 * objectives, records), f32),
             pltpu.VMEM((cells_x, width), f32),
             pltpu.VMEM((cells_x, width), f32),

time: 47.1 us -> 45.8 us (0.972)
  Pallas kernels: 46.2 us -> 44.9 us
    pallas_call x1, Pallas kernels: 46.2 us -> 44.9 us  [fused_shards(): pl.pallas_call(functools.partial(fused, n_px, n_py, cells_x), out_shape=p...]
where the time goes in v3:
time: 45.8 us; the launch traced here: 45.6 us
  Pallas kernels  44.9 us (98%)
  local copies, waits for them, and re-layouts  0.66 us (1%)
    pallas_call x1, Pallas kernels, fused_shards(): pl.pallas_call(functools.partial(fused, n_px, n_py, cells_x), out_shape=p...  44.9 us

profile of v3, /device:TPU:0, one launch (start us, length us, event | category | flops | bytes accessed | tf_op | source)
XLA Modules:
  0.0 45.6 jit_solution(11122727032693087563)
XLA Ops:
  0.0 44.9 %shard_map.82 = f32[2,8,16,128]{3,2,1,0:T(8,128)S(1)} custom-call(f32[2,8,16,128]{3,2,1,0:T(8,128)} %grad.1, f32[3,16,128]{2,1,0:T(8,128)} %coef.1, bf16[16,128,128]{2,1,0:T(8,128)(2,1)} %bitcast.4, bf16[4,4,128,128]{3,2,1,0:T(8,128)(2,1)} %bitcast.5, s32[1,256]{1,0:T(1,128)} %bitcast.6, s32[1,256]{1,0:T(1,128)} %bitcast.7, f32[2,256]{1,0:T(2,128)} %tile.1, ...), custom_call_target="tpu_custom_call" | custom-call | tf_op jit(solution)/shard_map/pallas_call | solution.py:515
  44.9 0.7 %copy.10 = f32[2,8,16,128]{3,2,1,0:T(8,128)} copy(f32[2,8,16,128]{3,2,1,0:T(8,128)S(1)} %shard_map.82) | data formatting | bytes 262144
